TPU v7x, 32 devices: a whole 2x2x4 slice. The times are simulated.
32 devices in a mesh: row: 8 (over z, x), col: 4 (over y, core).
Axes of the slice: x: 2, y: 2, z: 4, core: 2. Of those that a mesh axis runs over, the one named last changes fastest.
Arguments:
- right_side: float32 [384, 8192], P(None, ('row', 'col')), may hold values from -51 to 51
- leaf_inverse: float32 [32, 256, 256], P(('row', 'col')), may hold values from -0.375 to 0.375
- leaf_diag: float32 [32, 256, 256], P(('row', 'col')), may hold values from -0.375 to 0.375
- node_block: float32 [32, 256, 256], P(('row', 'col')), may hold values from -0.375 to 0.375
Outputs:
- solution: float32 [384, 8192], P(None, ('row', 'col'))
- residual_norm: float32 [384], replicated
All inputs are finite; a program needn't handle non-finite values.
Results may differ from a plain program's by a relative error of at most 0.0001.
Values sent between devices are 32-bit elements; how exact they have to be, the bound alone decides.
A program may use at most 64 MiB of HBM per device.

v0:
```python
import jax
import jax.numpy as jnp
from jax import lax
from jax.sharding import PartitionSpec as P

PRECISE = lax.Precision.HIGHEST


def swapped(block, axis, bit):
    count = lax.axis_size(axis)
    route = []
    for low in range(count):
        high = low | 1 << bit
        if high != low and high < count:
            route += [(low, high), (high, low)]
    return lax.ppermute(block, axis, route)


def apply_block(vectors, block):
    return lax.dot_general(
        vectors,
        block,
        (((1,), (1,)), ((), ())),
        precision=PRECISE,
        preferred_element_type=jnp.float32,
    )


def apply_transpose(vectors, block):
    return jnp.dot(vectors, block, precision=PRECISE, preferred_element_type=jnp.float32)


def bit_of(value, position):
    return value // 2**position % 2


def spread_all(block, device, holder_low, first_bit, last_bit):
    for position in range(first_bit, last_bit):
        partner = swapped(block, ("row", "col"), position)
        block = jnp.where(bit_of(device, position) == (holder_low >> position) % 2, block, partner)
    return block


def body(right_side, leaf_inverse, leaf_diag, node_block):
    devices = lax.axis_size("row") * lax.axis_size("col")
    tree_depth = devices.bit_length() - 1
    device = lax.axis_index("row") * lax.axis_size("col") + lax.axis_index("col")
    leaf_block = leaf_inverse[0]
    own_block = node_block[0]
    half_width = leaf_block.shape[0] // 2
    level_blocks = []
    for tree_level in range(1, tree_depth + 1):
        level_blocks.append(spread_all(own_block, device, 2 ** (tree_level - 1), 0, tree_level))
    root_block = spread_all(own_block, device, 0, 0, tree_depth)
    lifted = apply_block(right_side, leaf_block)
    leaf_part = lifted[:, :half_width]
    skeleton = lifted[:, half_width:]
    stored = []
    merged = lifted
    for tree_level in range(1, tree_depth + 1):
        partner = swapped(skeleton, ("row", "col"), tree_level - 1)
        is_left = bit_of(device, tree_level - 1) == 0
        left_part = jnp.where(is_left, skeleton, partner)
        right_part = jnp.where(is_left, partner, skeleton)
        merged = apply_block(
            jnp.concatenate([left_part, right_part], axis=1), level_blocks[tree_level - 1]
        )
        stored.append(merged[:, :half_width])
        skeleton = merged[:, half_width:]
    expanded = apply_block(merged, root_block)
    known = jnp.where(
        bit_of(device, tree_depth - 1) == 0, expanded[:, :half_width], expanded[:, half_width:]
    )
    for tree_level in range(tree_depth - 1, 0, -1):
        expanded = apply_transpose(
            jnp.concatenate([stored[tree_level - 1], known], axis=1), level_blocks[tree_level - 1]
        )
        known = jnp.where(
            bit_of(device, tree_level - 1) == 0, expanded[:, :half_width], expanded[:, half_width:]
        )
    solved = apply_transpose(jnp.concatenate([leaf_part, known], axis=1), leaf_block)
    residual = right_side - apply_block(solved, leaf_diag[0])
    totals = lax.psum(jnp.sum(residual * residual, axis=1), ("row", "col"))
    residual_norm = jnp.sqrt(totals / (devices * leaf_block.shape[0]) + 1e-06)
    return (solved, residual_norm)


def solution(mesh):
    return jax.shard_map(
        body,
        mesh=mesh,
        in_specs=(
            P(None, ("row", "col")),
            P(("row", "col"), None, None),
            P(("row", "col"), None, None),
            P(("row", "col"), None, None),
        ),
        out_specs=(P(None, ("row", "col")), P()),
        check_vma=False,
    )
```

profile of v0, /device:TPU:0, one launch (start us, length us, event | category | flops | bytes accessed | tf_op | source)
XLA Modules:
  0.0 117.6 jit_solution(12619264368154066166)
XLA Ops:
  0.6 0.9 copy-done
  1.6 1.6 %fusion.44 = f32[384,256]{0,1:T(8,128)S(1)} fusion(f32[384,256]{1,0:T(8,128)} %param.4, f32[1,256,256]{2,1,0:T(8,128)S(1)} %copy-done), kind=kOutput, calls=%fused_computation.45 | convolution fusion | flops 301989888 | bytes 1048576 | tf_op jit(solution)/shard_map/dot_general | solution.py:20
  6.4 2.9 %collective-permute-start.2 = (f32[384,128]{0,1:T(8,128)S(1)}, f32[384,128]{0,1:T(8,128)S(1)}, u32[]{:S(2)}, u32[]{:S(2)}) collective-permute-start(f32[384,128]{0,1:T(8,128)S(1)} %slice.83), channel_id=1, source_target_pairs={{0,2},{2,0},{1,3},{3,1},{4,6},{6,4},{5,7},{7,5},{8,10},{10,8},{9,1... | collective-permute-start | bytes 589832 | tf_op jit(solution)/shard_map/ppermute | solution.py:16
  9.5 5.6 %collective-permute-done.2 = f32[384,128]{0,1:T(8,128)S(1)} collective-permute-done((f32[384,128]{0,1:T(8,128)S(1)}, f32[384,128]{0,1:T(8,128)S(1)}, u32[]{:S(2)}, u32[]{:S(2)}) %collective-permute-start.2) | collective-permute-done | bytes 196640 | tf_op jit(solution)/shard_map/ppermute | solution.py:16
  15.8 4.4 %collective-permute-done.3 = f32[256,256]{1,0:T(8,128)S(1)} collective-permute-done((f32[256,256]{1,0:T(8,128)S(1)}, f32[256,256]{1,0:T(8,128)S(1)}, u32[]{:S(2)}, u32[]{:S(2)}) %collective-permute-start.3) | collective-permute-done | bytes 262176 | tf_op jit(solution)/shard_map/ppermute | solution.py:16
  20.8 1.8 %collective-permute-start.4 = (f32[384,128]{0,1:T(8,128)S(1)}, f32[384,128]{0,1:T(8,128)S(1)}, u32[]{:S(2)}, u32[]{:S(2)}) collective-permute-start(f32[384,128]{0,1:T(8,128)S(1)} %slice.85), channel_id=1, source_target_pairs={{0,4},{4,0},{1,5},{5,1},{2,6},{6,2},{3,7},{7,3},{8,12},{12,8},{9,1... | collective-permute-start | bytes 589832 | tf_op jit(solution)/shard_map/ppermute | solution.py:16
  23.0 5.6 %collective-permute-done.4 = f32[384,128]{0,1:T(8,128)S(1)} collective-permute-done((f32[384,128]{0,1:T(8,128)S(1)}, f32[384,128]{0,1:T(8,128)S(1)}, u32[]{:S(2)}, u32[]{:S(2)}) %collective-permute-start.4) | collective-permute-done | bytes 196640 | tf_op jit(solution)/shard_map/ppermute | solution.py:16
  29.4 3.5 %collective-permute-done.5 = f32[256,256]{1,0:T(8,128)S(1)} collective-permute-done((f32[256,256]{1,0:T(8,128)S(1)}, f32[256,256]{1,0:T(8,128)S(1)}, u32[]{:S(2)}, u32[]{:S(2)}) %collective-permute-start.5) | collective-permute-done | bytes 262176 | tf_op jit(solution)/shard_map/ppermute | solution.py:16
  33.5 1.6 %collective-permute-start.6 = (f32[384,128]{0,1:T(8,128)S(1)}, f32[384,128]{0,1:T(8,128)S(1)}, u32[]{:S(2)}, u32[]{:S(2)}) collective-permute-start(f32[384,128]{0,1:T(8,128)S(1)} %slice.87), channel_id=1, source_target_pairs={{0,8},{8,0},{1,9},{9,1},{2,10},{10,2},{3,11},{11,3},{4,12},{12,4},... | collective-permute-start | bytes 589832 | tf_op jit(solution)/shard_map/ppermute | solution.py:16
  35.7 5.6 %collective-permute-done.6 = f32[384,128]{0,1:T(8,128)S(1)} collective-permute-done((f32[384,128]{0,1:T(8,128)S(1)}, f32[384,128]{0,1:T(8,128)S(1)}, u32[]{:S(2)}, u32[]{:S(2)}) %collective-permute-start.6) | collective-permute-done | bytes 196640 | tf_op jit(solution)/shard_map/ppermute | solution.py:16
  42.1 2.6 %collective-permute-done.7 = f32[256,256]{1,0:T(8,128)S(1)} collective-permute-done((f32[256,256]{1,0:T(8,128)S(1)}, f32[256,256]{1,0:T(8,128)S(1)}, u32[]{:S(2)}, u32[]{:S(2)}) %collective-permute-start.7) | collective-permute-done | bytes 262176 | tf_op jit(solution)/shard_map/ppermute | solution.py:16
  46.0 2.2 %collective-permute-start.8 = (f32[384,128]{0,1:T(8,128)}, f32[384,128]{0,1:T(8,128)}, u32[]{:S(2)}, u32[]{:S(2)}) collective-permute-start(f32[384,128]{0,1:T(8,128)} %slice.89), channel_id=1, source_target_pairs={{0,16},{16,0},{1,17},{17,1},{2,18},{18,2},{3,19},{19,3},{4,20},{20... | collective-permute-start | bytes 589832 | tf_op jit(solution)/shard_map/ppermute | solution.py:16
  48.3 0.7 collective-permute-start.9
  49.1 0.9 copy.6
  50.0 12.2 %collective-permute-done.8 = f32[384,128]{0,1:T(8,128)} collective-permute-done((f32[384,128]{0,1:T(8,128)}, f32[384,128]{0,1:T(8,128)}, u32[]{:S(2)}, u32[]{:S(2)}) %collective-permute-start.8) | collective-permute-done | bytes 196640 | tf_op jit(solution)/shard_map/ppermute | solution.py:16
  62.2 1.0 broadcast_select_fusion.17
  63.2 4.2 %collective-permute-done.9 = f32[256,256]{1,0:T(8,128)} collective-permute-done((f32[256,256]{1,0:T(8,128)S(1)}, f32[256,256]{1,0:T(8,128)}, u32[]{:S(2)}, u32[]{:S(2)}) %collective-permute-start.9) | collective-permute-done | bytes 262176 | tf_op jit(solution)/shard_map/ppermute | solution.py:16
  67.4 1.8 %fusion.18 = f32[384,256]{1,0:T(8,128)S(1)} fusion(f32[384,128]{0,1:T(8,128)S(1)} %get-tuple-element.3, f32[384,128]{0,1:T(8,128)S(1)} %get-tuple-element.2, f32[256,256]{1,0:T(8,128)S(1)} %broadcast_select_fusion, f32[256,256]{1,0:T(8,128)} %collective-permute-done.9, pred[]{:T(512)S(6)} %eq.90), kind=kOutput, calls=%fused_computation.19 | convolution fusion | flops 302153728 | bytes 1310721 | tf_op jit(solution)/shard_map/dot_general | solution.py:20
  70.5 0.9 copy-done.8
  72.1 0.9 copy-done.7
  73.6 0.9 copy-done.6
  75.2 0.9 copy-done.5
  76.1 0.8 fusion.38
  77.9 39.1 %psum.7 = f32[384]{0:T(512)S(1)} all-reduce(f32[384]{0:T(512)S(1)} %fusion.1), channel_id=1, replica_groups=mesh['row'=8,'col'=4] {'row','col'}, use_global_device_ids=true, to_apply=%region_1.2 | all-reduce | flops 384 | bytes 3072 | tf_op jit(solution)/shard_map/psum | solution.py:83
  (51 shorter events, 14.0 us)
Async XLA Ops:
  0.6 1.0 copy-start
  3.2 1.0 copy-start.1
  3.2 1.6 %collective-permute-start = (f32[384,128]{0,1:T(8,128)S(1)}, f32[384,128]{0,1:T(8,128)S(1)}, u32[]{:S(2)}, u32[]{:S(2)}) collective-permute-start(f32[384,128]{0,1:T(8,128)S(1)} %slice.81), channel_id=1, source_target_pairs={{0,1},{1,0},{2,3},{3,2},{4,5},{5,4},{6,7},{7,6},{8,9},{9,8},{10,11... | collective-permute-start | bytes 589832 | tf_op jit(solution)/shard_map/ppermute | solution.py:16
  4.1 1.7 %collective-permute-start.1 = (f32[256,256]{1,0:T(8,128)S(1)}, f32[256,256]{1,0:T(8,128)S(1)}, u32[]{:S(2)}, u32[]{:S(2)}) collective-permute-start(f32[256,256]{1,0:T(8,128)S(1)} %bitcast.21), channel_id=1, source_target_pairs={{0,1},{1,0},{2,3},{3,2},{4,5},{5,4},{6,7},{7,6},{8,9},{9,8},{10,11... | collective-permute-start | bytes 786440 | tf_op jit(solution)/shard_map/ppermute | solution.py:16
  6.4 8.7 %collective-permute-start.2 = (f32[384,128]{0,1:T(8,128)S(1)}, f32[384,128]{0,1:T(8,128)S(1)}, u32[]{:S(2)}, u32[]{:S(2)}) collective-permute-start(f32[384,128]{0,1:T(8,128)S(1)} %slice.83), channel_id=1, source_target_pairs={{0,2},{2,0},{1,3},{3,1},{4,6},{6,4},{5,7},{7,5},{8,10},{10,8},{9,1... | collective-permute-start | bytes 589832 | tf_op jit(solution)/shard_map/ppermute | solution.py:16
  9.4 10.8 %collective-permute-start.3 = (f32[256,256]{1,0:T(8,128)S(1)}, f32[256,256]{1,0:T(8,128)S(1)}, u32[]{:S(2)}, u32[]{:S(2)}) collective-permute-start(f32[256,256]{1,0:T(8,128)S(1)} %broadcast_select_fusion.5), channel_id=1, source_target_pairs={{0,2},{2,0},{1,3},{3,1},{4,6},{6,4},{5,7},{7,5},{8,10},{10,8},{9,1... | collective-permute-start | bytes 786440 | tf_op jit(solution)/shard_map/ppermute | solution.py:16
  20.8 7.8 %collective-permute-start.4 = (f32[384,128]{0,1:T(8,128)S(1)}, f32[384,128]{0,1:T(8,128)S(1)}, u32[]{:S(2)}, u32[]{:S(2)}) collective-permute-start(f32[384,128]{0,1:T(8,128)S(1)} %slice.85), channel_id=1, source_target_pairs={{0,4},{4,0},{1,5},{5,1},{2,6},{6,2},{3,7},{7,3},{8,12},{12,8},{9,1... | collective-permute-start | bytes 589832 | tf_op jit(solution)/shard_map/ppermute | solution.py:16
  22.6 10.2 %collective-permute-start.5 = (f32[256,256]{1,0:T(8,128)S(1)}, f32[256,256]{1,0:T(8,128)S(1)}, u32[]{:S(2)}, u32[]{:S(2)}) collective-permute-start(f32[256,256]{1,0:T(8,128)S(1)} %broadcast_select_fusion.3), channel_id=1, source_target_pairs={{0,4},{4,0},{1,5},{5,1},{2,6},{6,2},{3,7},{7,3},{8,12},{12,8},{9,1... | collective-permute-start | bytes 786440 | tf_op jit(solution)/shard_map/ppermute | solution.py:16
  33.5 7.8 %collective-permute-start.6 = (f32[384,128]{0,1:T(8,128)S(1)}, f32[384,128]{0,1:T(8,128)S(1)}, u32[]{:S(2)}, u32[]{:S(2)}) collective-permute-start(f32[384,128]{0,1:T(8,128)S(1)} %slice.87), channel_id=1, source_target_pairs={{0,8},{8,0},{1,9},{9,1},{2,10},{10,2},{3,11},{11,3},{4,12},{12,4},... | collective-permute-start | bytes 589832 | tf_op jit(solution)/shard_map/ppermute | solution.py:16
  35.1 9.6 %collective-permute-start.7 = (f32[256,256]{1,0:T(8,128)S(1)}, f32[256,256]{1,0:T(8,128)S(1)}, u32[]{:S(2)}, u32[]{:S(2)}) collective-permute-start(f32[256,256]{1,0:T(8,128)S(1)} %broadcast_select_fusion.1), channel_id=1, source_target_pairs={{0,8},{8,0},{1,9},{9,1},{2,10},{10,2},{3,11},{11,3},{4,12},{12,4},... | collective-permute-start | bytes 786440 | tf_op jit(solution)/shard_map/ppermute | solution.py:16
  46.0 3.0 %copy-start.2 = (f32[384,256]{1,0:T(8,128)S(1)}, f32[384,256]{1,0:T(8,128)}, u32[]{:S(2)}) copy-start(f32[384,256]{1,0:T(8,128)} %param.4) | copy-start | bytes 1179652
  46.0 16.2 %collective-permute-start.8 = (f32[384,128]{0,1:T(8,128)}, f32[384,128]{0,1:T(8,128)}, u32[]{:S(2)}, u32[]{:S(2)}) collective-permute-start(f32[384,128]{0,1:T(8,128)} %slice.89), channel_id=1, source_target_pairs={{0,16},{16,0},{1,17},{17,1},{2,18},{18,2},{3,19},{19,3},{4,20},{20... | collective-permute-start | bytes 589832 | tf_op jit(solution)/shard_map/ppermute | solution.py:16
  48.3 19.0 %collective-permute-start.9 = (f32[256,256]{1,0:T(8,128)S(1)}, f32[256,256]{1,0:T(8,128)}, u32[]{:S(2)}, u32[]{:S(2)}) collective-permute-start(f32[256,256]{1,0:T(8,128)S(1)} %broadcast_select_fusion), channel_id=1, source_target_pairs={{0,16},{16,0},{1,17},{17,1},{2,18},{18,2},{3,19},{19,3},{4,20},{20... | collective-permute-start | bytes 786440 | tf_op jit(solution)/shard_map/ppermute | solution.py:16
  70.4 0.9 copy-start.8
  72.0 0.9 copy-start.7
  73.6 0.9 copy-start.6
  75.2 0.9 copy-start.5
  76.1 1.0 copy-start.3
  76.1 1.1 copy-start.9
  77.2 0.7 copy-start.4
where the time goes:
time: 118 us
  waiting for transfers between devices  44.2 us (37%)
  blocking collectives  39.1 us (33%)
  starting transfers between devices  11.4 us (10%)
  matrix products  10.4 us (9%)
  local copies, waits for them, and re-layouts  6.92 us (6%)
  other arithmetic  4.66 us (4%)
    ppermute x10, waiting for transfers between devices, swapped(): return lax.ppermute(block, axis, route)  44.2 us
    psum x1, blocking collectives, body(): totals = lax.psum(jnp.sum(residual * residual, axis=1), ('row', 'col'))  39.1 us
    ppermute x10, starting transfers between devices, swapped(): return lax.ppermute(block, axis, route)  11.4 us
    dot_general x8, matrix products, apply_block(): lax.dot_general(vectors, block, (((1,), (1,)), ((), ())), precision=PRECI...  7.02 us
    unnamed x21, local copies, waits for them, and re-layouts  6.16 us
    select_n x5, other arithmetic, body(): left_part = jnp.where(is_left, skeleton, partner)  3.82 us
    dot_general x5, matrix products, apply_transpose(): jnp.dot(vectors, block, precision=PRECISE, preferred_element_type=jnp.flo...  3.4 us
  transfers between devices with their start and end apart: 10, of which 10 were waited for; matrix products, arithmetic and copies ran while one was open for 4% of the time, Pallas kernels for 0%

commit v1 on v0

v1 whole, which is shorter than its diff:
```python
import functools

import jax
import jax.numpy as jnp
from jax import lax
from jax.experimental import pallas as pl
from jax.experimental.pallas import tpu as pltpu
from jax.sharding import PartitionSpec as P

MESH = pl.DeviceIdType.MESH
CHUNKS = 2
GROUP_BITS = 3


def halves(value):
    high = value.astype(jnp.bfloat16)
    low = (value - high.astype(jnp.float32)).astype(jnp.bfloat16)
    return high, low


def product(vectors, block, contract):
    rows = vectors.shape[0]
    high, low = halves(vectors)
    block_high, block_low = halves(block)
    dims = (((1,), (contract,)), ((), ()))
    both = lax.dot_general(
        jnp.concatenate([high, low], axis=0), block_high, dims, preferred_element_type=jnp.float32
    )
    cross = lax.dot_general(high, block_low, dims, preferred_element_type=jnp.float32)
    return both[:rows] + (both[rows:] + cross)


def apply_block(vectors, block):
    return product(vectors, block, 1)


def apply_transpose(vectors, block):
    return product(vectors, block, 0)


def kernel(devices, columns, sharded, *refs):
    depth = devices.bit_length() - 1
    (rhs_hbm, leaf_hbm, diag_hbm, node_hbm, out_hbm, norm_ref) = refs[:6]
    (rhs, leaf, diag, solved, blocks, leaf_e, parts, sums) = refs[6:14]
    rest = list(refs[14:])
    skeletons = [rest.pop(0) for _ in range(depth)]
    arrived = [None] + [rest.pop(0) for _ in range(depth)]
    stored = [None] + [rest.pop(0) for _ in range(depth - 1)]
    known_rows = [rest.pop(0) for _ in range(sharded)]
    outgoing = [None] + [rest.pop(0) for _ in range(sharded)]
    (local, block_send, block_recv, up_send, up_recv, down_send, down_recv, sum_send, sum_recv) = rest

    total_rows, width = rhs.shape
    half = width // 2
    chunk = width // CHUNKS
    me = lax.axis_index("row") * columns + lax.axis_index("col")

    def bit(position):
        return lax.rem(lax.div(me, 2**position), 2)

    def place(index):
        return (lax.div(index, columns), lax.rem(index, columns))

    def flipped(delta):
        other = me
        for position in range(depth):
            if delta >> position & 1:
                other = other + (1 - 2 * bit(position)) * 2**position
        return place(other)

    groups = []
    for first in range(0, depth, GROUP_BITS):
        groups.append((first, min(GROUP_BITS, depth - first)))
    deltas = [(g, d, d << first) for g, (first, size) in enumerate(groups) for d in range(1, 2**size)]

    slot = jnp.int32(0)
    for position in range(depth):
        slot = jnp.where(lax.rem(me, 2 ** (position + 1)) == 2**position, position + 1, slot)
    load_node = pltpu.make_async_copy(node_hbm.at[0], blocks.at[slot], local.at[0])
    load_leaf = pltpu.make_async_copy(leaf_hbm.at[0], leaf, local.at[1])
    load_rhs = pltpu.make_async_copy(rhs_hbm, rhs, local.at[2])
    load_diag = pltpu.make_async_copy(diag_hbm.at[0], diag, local.at[3])
    load_node.start()
    load_leaf.start()
    load_rhs.start()
    load_diag.start()

    barrier = pltpu.get_barrier_semaphore()
    for _, _, delta in deltas:
        pl.semaphore_signal(barrier, inc=1, device_id=flipped(delta), device_id_type=MESH)

    def sends(level, position):
        if level == 0:
            return me == 0
        if position == level - 1:
            return lax.rem(me, 2**level) == 2 ** (level - 1)
        return lax.rem(me, 2 ** (position + 1)) == 0

    def receives(level, position):
        if level == 0:
            return me == devices // 2
        if position == level - 1:
            return lax.rem(me, 2**level) == 0
        return lax.rem(me, 2 ** (position + 1)) == 2**position

    def block_copy(level, position, piece):
        return pltpu.make_async_remote_copy(
            src_ref=blocks.at[level, pl.ds(piece * chunk, chunk)],
            dst_ref=blocks.at[level, pl.ds(piece * chunk, chunk)],
            send_sem=block_send.at[level, position, piece],
            recv_sem=block_recv.at[level, piece],
            device_id=flipped(1 << position),
            device_id_type=MESH,
        )

    moves = []

    def block_start(level, position, piece):
        moves.append((level, position, piece))

        @pl.when(sends(level, position))
        def _():
            block_copy(level, position, piece).start()

    def block_wait(level, position, piece):
        @pl.when(receives(level, position))
        def _():
            block_copy(level, position, piece).wait_recv()

    def relay(phase):
        for piece in range(CHUNKS):
            for level in range(phase, depth):
                position = level - phase
                if phase > 1:
                    block_wait(level, position + 1, piece)
                block_start(level, position, piece)
        if phase == 1:
            for piece in range(CHUNKS):
                block_start(0, depth - 1, piece)
                block_start(depth, depth - 1, piece)
        if phase == 2:
            for piece in range(CHUNKS):
                block_wait(0, depth - 1, piece)
                block_wait(depth, depth - 1, piece)

            @pl.when(lax.rem(me, devices // 2) == 0)
            def _():
                blocks[depth + 1] = apply_transpose(blocks[0], blocks[depth])

            for piece in range(CHUNKS):
                block_start(depth + 1, depth - 2, piece)
        if phase > 2:
            for piece in range(CHUNKS):
                position = depth - phase
                block_wait(depth + 1, position + 1, piece)
                block_start(depth + 1, position, piece)

    def rows_at(level):
        return total_rows // 2 ** min(level, sharded)

    def span(side, size):
        return pl.ds(pl.multiple_of(side * size, size), size)

    def up_copy(level):
        if level <= sharded:
            source = skeletons[level - 1].at[span(1 - bit(level - 1), rows_at(level))]
        else:
            source = skeletons[level - 1]
        return pltpu.make_async_remote_copy(
            src_ref=source,
            dst_ref=arrived[level],
            send_sem=up_send.at[level],
            recv_sem=up_recv.at[level],
            device_id=flipped(1 << (level - 1)),
            device_id_type=MESH,
        )

    def joined(level):
        if level <= sharded:
            own = skeletons[level - 1][span(bit(level - 1), rows_at(level)), :]
        else:
            own = skeletons[level - 1][...]
        other = arrived[level][...]
        left = bit(level - 1) == 0
        return jnp.concatenate(
            [jnp.where(left, own, other), jnp.where(left, other, own)], axis=1
        )

    def down_copy(level):
        size = rows_at(level)
        return pltpu.make_async_remote_copy(
            src_ref=outgoing[level],
            dst_ref=known_rows[level - 1].at[span(bit(level - 1), size)],
            send_sem=down_send.at[level],
            recv_sem=down_recv.at[level],
            device_id=flipped(1 << (level - 1)),
            device_id_type=MESH,
        )

    load_node.wait()
    pl.semaphore_wait(barrier, len(deltas))
    relay(1)
    load_leaf.wait()
    load_rhs.wait()
    first = span(1 - bit(0), total_rows // 2)
    second = span(bit(0), total_rows // 2)
    skeletons[0][first, :] = apply_block(rhs[first, :], leaf[half:, :])
    up_copy(1).start()
    skeletons[0][second, :] = apply_block(rhs[second, :], leaf[half:, :])
    relay(2)
    leaf_e[...] = apply_block(rhs[...], leaf[:half, :])

    for level in range(1, depth):
        if level > 1:
            relay(level + 1)
        for piece in range(CHUNKS):
            block_wait(level, 0, piece)
        up_copy(level).wait_recv()
        merged = apply_block(joined(level), blocks[level])
        skeletons[level][...] = merged[:, half:]
        up_copy(level + 1).start()
        stored[level][...] = merged[:, :half]

    for piece in range(CHUNKS):
        block_wait(depth + 1, 0, piece)
    up_copy(depth).wait_recv()
    known = apply_block(joined(depth), blocks[depth + 1, span(bit(depth - 1), half), :])
    for level in range(depth - 1, sharded, -1):
        known = apply_transpose(
            jnp.concatenate([stored[level][...], known], axis=1),
            blocks[level, :, span(bit(level - 1), half)],
        )
    for level in range(sharded, 0, -1):
        if level < sharded:
            down_copy(level + 1).wait_recv()
            known = known_rows[level][...]
        expanded = apply_transpose(
            jnp.concatenate([stored[level][...], known], axis=1), blocks[level]
        )
        left = bit(level - 1) == 0
        outgoing[level][...] = jnp.where(left, expanded[:, half:], expanded[:, :half])
        down_copy(level).start()
        known_rows[level - 1][span(bit(level - 1), rows_at(level)), :] = jnp.where(
            left, expanded[:, :half], expanded[:, half:]
        )

    ones = jnp.ones((8, width), jnp.bfloat16)
    store_out = []
    load_diag.wait()
    totals = []
    for index, rows in enumerate((second, first)):
        if index == 1:
            down_copy(1).wait_recv()
        result = apply_transpose(
            jnp.concatenate([leaf_e[rows, :], known_rows[0][rows, :]], axis=1), leaf[...]
        )
        solved[rows, :] = result
        store = pltpu.make_async_copy(solved.at[rows], out_hbm.at[rows], local.at[4 + index])
        store.start()
        store_out.append(store)
        residual = rhs[rows, :] - apply_block(result, diag[...])
        high, low = halves(residual * residual)
        dims = (((1,), (1,)), ((), ()))
        totals.append(
            lax.dot_general(ones, high, dims, preferred_element_type=jnp.float32)
            + lax.dot_general(ones, low, dims, preferred_element_type=jnp.float32)
        )
    is_even = bit(0) == 0
    total = jnp.concatenate(
        [jnp.where(is_even, totals[0], totals[1]), jnp.where(is_even, totals[1], totals[0])], axis=1
    )[:1]

    def sum_copy(group, delta):
        position, size = groups[group]
        mine = lax.rem(lax.div(me, 2**position), 2**size)
        return pltpu.make_async_remote_copy(
            src_ref=sums.at[group],
            dst_ref=parts.at[group, mine],
            send_sem=sum_send.at[group, delta],
            recv_sem=sum_recv.at[group, delta],
            device_id=flipped(delta << position),
            device_id_type=MESH,
        )

    for group, (position, size) in enumerate(groups):
        mine = lax.rem(lax.div(me, 2**position), 2**size)
        sums[group] = total
        for delta in range(1, 2**size):
            sum_copy(group, delta).start()
        parts[group, mine] = total
        for delta in range(1, 2**size):
            sum_copy(group, delta).wait_recv()
        total = parts[group, 0]
        for member in range(1, 2**size):
            total = total + parts[group, member]
    norm_ref[...] = jnp.sqrt(total / (devices * width) + 1e-06)

    for level, position, piece in moves:

        @pl.when(sends(level, position))
        def _(level=level, position=position, piece=piece):
            block_copy(level, position, piece).wait_send()

    for level in range(1, depth + 1):
        up_copy(level).wait_send()
    for level in range(1, sharded + 1):
        down_copy(level).wait_send()
    for group, delta, _ in deltas:
        sum_copy(group, delta).wait_send()
    for store in store_out:
        store.wait()


def body(right_side, leaf_inverse, leaf_diag, node_block):
    columns = lax.axis_size("col")
    devices = lax.axis_size("row") * columns
    depth = devices.bit_length() - 1
    rows, width = right_side.shape
    half = width // 2
    sharded = 1
    while sharded < depth - 1 and sharded < 3 and rows % (2 ** (sharded + 1) * 16) == 0:
        sharded += 1
    groups = -(-depth // GROUP_BITS)

    def rows_at(level):
        return rows // 2 ** min(level, sharded)

    def vmem(*shape):
        return pltpu.VMEM(shape, jnp.float32)

    dma = pltpu.SemaphoreType.DMA
    scratch = [
        vmem(rows, width),
        vmem(width, width),
        vmem(width, width),
        vmem(rows, width),
        vmem(depth + 2, width, width),
        vmem(rows, half),
        vmem(groups, 2**GROUP_BITS, 1, rows),
        vmem(groups, 1, rows),
    ]
    scratch += [vmem(rows_at(level), half) for level in range(depth)]
    scratch += [vmem(rows_at(level), half) for level in range(1, depth + 1)]
    scratch += [vmem(rows_at(level), half) for level in range(1, depth)]
    scratch += [vmem(rows_at(level), half) for level in range(sharded)]
    scratch += [vmem(rows_at(level), half) for level in range(1, sharded + 1)]
    scratch += [
        dma((6,)),
        dma((depth + 2, depth, CHUNKS)),
        dma((depth + 2, CHUNKS)),
        dma((depth + 1,)),
        dma((depth + 1,)),
        dma((sharded + 1,)),
        dma((sharded + 1,)),
        dma((groups, 2**GROUP_BITS)),
        dma((groups, 2**GROUP_BITS)),
    ]
    anywhere = pl.BlockSpec(memory_space=pl.ANY)
    solved, norm = pl.pallas_call(
        functools.partial(kernel, devices, columns, sharded),
        out_shape=(
            jax.ShapeDtypeStruct((rows, width), jnp.float32),
            jax.ShapeDtypeStruct((1, rows), jnp.float32),
        ),
        in_specs=[anywhere] * 4,
        out_specs=(anywhere, pl.BlockSpec(memory_space=pltpu.VMEM)),
        scratch_shapes=scratch,
        compiler_params=pltpu.CompilerParams(collective_id=0, has_side_effects=True),
    )(right_side, leaf_inverse, leaf_diag, node_block)
    return (solved, norm.reshape(rows))


def solution(mesh):
    return jax.shard_map(
        body,
        mesh=mesh,
        in_specs=(
            P(None, ("row", "col")),
            P(("row", "col"), None, None),
            P(("row", "col"), None, None),
            P(("row", "col"), None, None),
        ),
        out_specs=(P(None, ("row", "col")), P()),
        check_vma=False,
    )
```

time: 118 us -> 49.4 us (0.42)
  Pallas kernels: 0 us -> 45.6 us
  waiting for transfers between devices: 44.2 us -> 0 us
  blocking collectives: 39.1 us -> 0 us
  starting transfers between devices: 11.4 us -> 0 us
  matrix products: 10.4 us -> 0 us
  local copies, waits for them, and re-layouts: 6.92 us -> 2.43 us
  other arithmetic: 4.66 us -> 0.6 us
    pallas_call x0 -> x1, Pallas kernels: none -> 45.6 us  [body(): pl.pallas_call(functools.partial(kernel, devices, columns, sharded), out_...]
    ppermute x10 -> x0, waiting for transfers between devices: 44.2 us -> none  [swapped(): return lax.ppermute(block, axis, route)]
    psum x1 -> x0, blocking collectives: 39.1 us -> none  [body(): totals = lax.psum(jnp.sum(residual * residual, axis=1), ('row', 'col'))]
    ppermute x10 -> x0, starting transfers between devices: 11.4 us -> none  [swapped(): return lax.ppermute(block, axis, route)]
    dot_general x13 -> x0, matrix products: 10.4 us -> none  [the longest x8 7.02 us: apply_block(): lax.dot_general(vectors, block, (((1,), (1,)), ((), ())), precision=PRECI...]
    select_n x14 -> x0, other arithmetic: 4.07 us -> none  [the longest x5 3.82 us: body(): left_part = jnp.where(is_left, skeleton, partner)]
    unnamed x21 -> x3, local copies, waits for them, and re-layouts: 6.16 us -> 2.43 us
  transfers between devices with their start and end apart: 10 -> 0, of which waited for: 10 -> 0; matrix products, arithmetic and copies ran while one was open for 4% -> 0% of each run, Pallas kernels for 0% -> 0%
where the time goes in v1:
time: 49.4 us; the launch traced here: 49.2 us
  Pallas kernels  45.6 us (92%)
  local copies, waits for them, and re-layouts  2.43 us (5%)
  between operations  0.65 us (1%)
  other arithmetic  0.6 us (1%)
    pallas_call x1, Pallas kernels, body(): pl.pallas_call(functools.partial(kernel, devices, columns, sharded), out_...  45.6 us
    unnamed x3, local copies, waits for them, and re-layouts  2.43 us

profile of v1, /device:TPU:0, one launch (start us, length us, event | category | flops | bytes accessed | tf_op | source)
XLA Modules:
  0.0 49.2 jit_solution(17963979849749349365)
XLA Ops:
  0.6 45.6 %shard_map.59 = (f32[384,256]{1,0:T(8,128)}, f32[1,384]{1,0:T(1,128)}) custom-call(f32[384,256]{1,0:T(8,128)} %refs_0_.1, f32[1,256,256]{2,1,0:T(8,128)} %refs_1_.1, f32[1,256,256]{2,1,0:T(8,128)} %refs_2_.1, f32[1,256,256]{2,1,0:T(8,128)} %refs_3_.1), custom_call_target="tpu_custom_call" | custom-call | tf_op jit(solution)/shard_map/pallas_call | solution.py:359
  46.2 0.0 copy-start
  46.2 0.7 %copy-done = f32[1,384]{1,0:T(1,128)S(1)} copy-done((f32[1,384]{1,0:T(1,128)S(1)}, f32[1,384]{1,0:T(1,128)}, u32[]{:S(2)}) %copy-start) | copy-done | bytes 1560
  46.9 0.6 %reduce = f32[384]{0:T(512)} reduce(f32[1,384]{1,0:T(1,128)S(1)} %copy-done, f32[]{:T(128)} %constant.3), dimensions={0}, to_apply=%get-tuple-element.5.reduce_sub_computation | reduce | bytes 3076 | tf_op jit(solution)/shard_map/pallas_call | solution.py:359
  47.5 1.8 %copy.7 = f32[384,256]{1,0:T(8,128)} copy(f32[384,256]{1,0:T(8,128)} %get-tuple-element.8) | data formatting | bytes 786432
Async XLA Ops:
  46.2 0.7 %copy-start = (f32[1,384]{1,0:T(1,128)S(1)}, f32[1,384]{1,0:T(1,128)}, u32[]{:S(2)}) copy-start(f32[1,384]{1,0:T(1,128)} %get-tuple-element.5) | copy-start | bytes 4612

commit v2 on v1

v2 whole, which is shorter than its diff:
```python
import functools

import jax
import jax.numpy as jnp
from jax import lax
from jax.experimental import pallas as pl
from jax.experimental.pallas import tpu as pltpu
from jax.sharding import PartitionSpec as P

MESH = pl.DeviceIdType.MESH
PIECES = 1
GROUP_BITS = 5
STREAMS = 1
SHARDED = 1


def halves(value):
    high = value.astype(jnp.bfloat16)
    low = (value - high.astype(jnp.float32)).astype(jnp.bfloat16)
    return high, low


def product(vectors, block, contract):
    rows = vectors.shape[0]
    high, low = halves(vectors)
    block_high, block_low = block
    dims = (((1,), (contract,)), ((), ()))
    both = lax.dot_general(
        jnp.concatenate([high, low], axis=0), block_high, dims, preferred_element_type=jnp.float32
    )
    cross = lax.dot_general(high, block_low, dims, preferred_element_type=jnp.float32)
    return both[:rows] + (both[rows:] + cross)


def apply_block(vectors, block):
    return product(vectors, halves(block), 1)


def apply_transpose(vectors, block):
    return product(vectors, halves(block), 0)


def kernel(devices, columns, sharded, *refs):
    depth = devices.bit_length() - 1
    (rhs_hbm, leaf_hbm, diag_hbm, node_hbm, solved, norm_ref) = refs[:6]
    (rhs, leaf, diag, blocks, leaf_e, parts, sums) = refs[6:13]
    rest = list(refs[13:])
    skeletons = [rest.pop(0) for _ in range(depth)]
    arrived = [None] + [rest.pop(0) for _ in range(depth)]
    stored = [None] + [rest.pop(0) for _ in range(depth - 1)]
    known_rows = [rest.pop(0) for _ in range(sharded)]
    outgoing = [None] + [rest.pop(0) for _ in range(sharded)]
    (local, block_send, block_recv, up_send, up_recv, down_send, down_recv, sum_send, sum_recv) = rest

    total_rows, width = rhs.shape
    half = width // 2
    chunk = half // PIECES
    upper, lower = range(PIECES), range(PIECES, 2 * PIECES)
    me = lax.axis_index("row") * columns + lax.axis_index("col")

    def bit(position):
        return lax.rem(lax.div(me, 2**position), 2)

    def place(index):
        return (lax.div(index, columns), lax.rem(index, columns))

    def flipped(delta):
        other = me
        for position in range(depth):
            if delta >> position & 1:
                other = other + (1 - 2 * bit(position)) * 2**position
        return place(other)

    groups = []
    for first in range(0, depth, GROUP_BITS):
        groups.append((first, min(GROUP_BITS, depth - first)))
    deltas = [(g, d, d << first) for g, (first, size) in enumerate(groups) for d in range(1, 2**size)]

    slot = jnp.int32(0)
    for position in range(depth):
        slot = jnp.where(lax.rem(me, 2 ** (position + 1)) == 2**position, position + 1, slot)
    load_node = pltpu.make_async_copy(node_hbm.at[0], blocks.at[slot], local.at[0])
    load_leaf = pltpu.make_async_copy(leaf_hbm.at[0], leaf, local.at[1])
    load_rhs = pltpu.make_async_copy(rhs_hbm, rhs, local.at[2])
    load_diag = pltpu.make_async_copy(diag_hbm.at[0], diag, local.at[3])
    load_node.start()
    load_leaf.start()
    load_rhs.start()
    load_diag.start()

    barrier = pltpu.get_barrier_semaphore()
    for position in range(depth):
        pl.semaphore_signal(
            barrier, inc=1, device_id=flipped(1 << position), device_id_type=MESH
        )

    def sends(level, position):
        if level == 0:
            return me == 0
        if position == level - 1:
            return lax.rem(me, 2**level) == 2 ** (level - 1)
        return lax.rem(me, 2 ** (position + 1)) == 0

    def receives(level, position):
        if level == 0:
            return me == devices // 2
        if position == level - 1:
            return lax.rem(me, 2**level) == 0
        return lax.rem(me, 2 ** (position + 1)) == 2**position

    def block_copy(level, position, piece):
        rows = pl.ds(piece * chunk, chunk)
        return pltpu.make_async_remote_copy(
            src_ref=blocks.at[level, rows],
            dst_ref=blocks.at[level, rows],
            send_sem=block_send.at[level, position, piece],
            recv_sem=block_recv.at[level, piece],
            device_id=flipped(1 << position),
            device_id_type=MESH,
        )

    moves = []

    def block_start(level, position, piece):
        moves.append((level, position, piece))

        @pl.when(sends(level, position))
        def _():
            block_copy(level, position, piece).start()

    def block_wait(level, position, piece):
        @pl.when(receives(level, position))
        def _():
            block_copy(level, position, piece).wait_recv()

    def relay(phase, pieces):
        for piece in pieces:
            for level in range(phase, depth):
                position = level - phase
                if phase > 1:
                    block_wait(level, position + 1, piece)
                block_start(level, position, piece)

    def relay_root(phase):
        if phase == 1:
            for piece in (*upper, *lower):
                block_start(depth, depth - 1, piece)
            for piece in lower:
                block_start(0, depth - 1, piece)
            return
        if phase == 2:
            for piece in (*upper, *lower):
                block_wait(depth, depth - 1, piece)
            for piece in lower:
                block_wait(0, depth - 1, piece)

            @pl.when(lax.rem(me, devices // 2) == 0)
            def _():
                blocks[depth + 1, :half] = apply_transpose(
                    blocks[0, span(bit(depth - 1), half)], blocks[depth]
                )

        for piece in upper:
            position = depth - phase
            if phase > 2:
                block_wait(depth + 1, position + 1, piece)
            block_start(depth + 1, position, piece)

    def rows_at(level):
        return total_rows // 2 ** min(level, sharded)

    def span(side, size):
        return pl.ds(pl.multiple_of(side * size, size), size)

    def stream(level, index, side=None):
        size = rows_at(level) // STREAMS
        if side is None:
            return pl.ds(index * size, size)
        return pl.ds(pl.multiple_of(side * rows_at(level) + index * size, 8), size)

    def side_of(level):
        return bit(level - 1) if level <= sharded else None

    def other_side(level):
        return 1 - bit(level - 1) if level <= sharded else None

    def up_copy(level, index):
        return pltpu.make_async_remote_copy(
            src_ref=skeletons[level - 1].at[stream(level, index, other_side(level))],
            dst_ref=arrived[level].at[stream(level, index)],
            send_sem=up_send.at[level, index],
            recv_sem=up_recv.at[level, index],
            device_id=flipped(1 << (level - 1)),
            device_id_type=MESH,
        )

    def joined(level, index):
        own = skeletons[level - 1][stream(level, index, side_of(level)), :]
        other = arrived[level][stream(level, index), :]
        left = bit(level - 1) == 0
        return jnp.concatenate(
            [jnp.where(left, own, other), jnp.where(left, other, own)], axis=1
        )

    def down_copy(level, index):
        return pltpu.make_async_remote_copy(
            src_ref=outgoing[level].at[stream(level, index)],
            dst_ref=known_rows[level - 1].at[stream(level, index, bit(level - 1))],
            send_sem=down_send.at[level, index],
            recv_sem=down_recv.at[level, index],
            device_id=flipped(1 << (level - 1)),
            device_id_type=MESH,
        )

    load_node.wait()
    pl.semaphore_wait(barrier, depth)
    relay(1, lower)
    relay_root(1)
    load_leaf.wait()
    load_rhs.wait()
    lift = halves(leaf[half:, :])
    for index in range(STREAMS):
        rows = stream(1, index, other_side(1))
        skeletons[0][rows, :] = product(rhs[rows, :], lift, 1)
        up_copy(1, index).start()
    for index in range(STREAMS):
        rows = stream(1, index, side_of(1))
        skeletons[0][rows, :] = product(rhs[rows, :], lift, 1)
    leaf_e[...] = apply_block(rhs[...], leaf[:half, :])

    def keep(level):
        for piece in upper:
            block_wait(level, 0, piece)
        weights = halves(blocks[level, :half])
        for index in range(STREAMS):
            stored[level][stream(level, index), :] = product(joined(level, index), weights, 1)

    for level in range(1, depth):
        for piece in lower:
            block_wait(level, 0, piece)
        weights = halves(blocks[level, half:])
        for index in range(STREAMS):
            up_copy(level, index).wait_recv()
            result = product(joined(level, index), weights, 1)
            skeletons[level][stream(level, index), :] = result
            if level >= sharded:
                up_copy(level + 1, index).start()
        if level < sharded:
            for index in range(STREAMS):
                up_copy(level + 1, index).start()
        relay(level + 1, lower)
        relay(level, upper)
        relay_root(level + 1)
        if level > 1:
            keep(level - 1)
    keep(depth - 1)

    for piece in upper:
        block_wait(depth + 1, 0, piece)
    root_weights = halves(blocks[depth + 1, :half])
    above = {
        level: halves(blocks[level, :, span(bit(level - 1), half)])
        for level in range(depth - 1, sharded, -1)
    }

    def lower_rows(level, index, known, weights):
        joint = jnp.concatenate([stored[level][stream(level, index), :], known], axis=1)
        expanded = product(joint, weights, 0)
        left = bit(level - 1) == 0
        outgoing[level][stream(level, index), :] = jnp.where(
            left, expanded[:, half:], expanded[:, :half]
        )
        down_copy(level, index).start()
        known_rows[level - 1][stream(level, index, bit(level - 1)), :] = jnp.where(
            left, expanded[:, :half], expanded[:, half:]
        )

    weights = halves(blocks[sharded])
    for index in range(STREAMS):
        up_copy(depth, index).wait_recv()
        known = product(joined(depth, index), root_weights, 1)
        for level in range(depth - 1, sharded, -1):
            joint = jnp.concatenate([stored[level][stream(level, index), :], known], axis=1)
            known = product(joint, above[level], 0)
        lower_rows(sharded, index, known, weights)
    for level in range(sharded - 1, 0, -1):
        weights = halves(blocks[level])
        for index in range(STREAMS):
            down_copy(level + 1, index).wait_recv()
        for index in range(STREAMS):
            lower_rows(level, index, known_rows[level][stream(level, index), :], weights)

    ones = jnp.ones((8, width), jnp.bfloat16)
    load_diag.wait()
    leaf_weights = halves(leaf[...])
    diag_weights = halves(diag[...])
    totals = []
    for mine in (True, False):
        squares = []
        for index in range(STREAMS):
            rows = stream(1, index, side_of(1) if mine else other_side(1))
            if not mine:
                down_copy(1, index).wait_recv()
            joint = jnp.concatenate([leaf_e[rows, :], known_rows[0][rows, :]], axis=1)
            result = product(joint, leaf_weights, 0)
            solved[rows, :] = result
            residual = rhs[rows, :] - product(result, diag_weights, 1)
            squares.append(residual * residual)
        high, low = halves(jnp.concatenate(squares, axis=0))
        dims = (((1,), (1,)), ((), ()))
        totals.append(
            lax.dot_general(ones, high, dims, preferred_element_type=jnp.float32)
            + lax.dot_general(ones, low, dims, preferred_element_type=jnp.float32)
        )
    is_even = bit(0) == 0
    total = jnp.concatenate(
        [jnp.where(is_even, totals[0], totals[1]), jnp.where(is_even, totals[1], totals[0])], axis=1
    )[:1]

    def sum_copy(group, delta):
        position, size = groups[group]
        mine = lax.rem(lax.div(me, 2**position), 2**size)
        return pltpu.make_async_remote_copy(
            src_ref=sums.at[group],
            dst_ref=parts.at[group, mine],
            send_sem=sum_send.at[group, delta],
            recv_sem=sum_recv.at[group, delta],
            device_id=flipped(delta << position),
            device_id_type=MESH,
        )

    for group, (position, size) in enumerate(groups):
        mine = lax.rem(lax.div(me, 2**position), 2**size)
        sums[group] = total
        for delta in range(1, 2**size):
            sum_copy(group, delta).start()
        parts[group, mine] = total
        for delta in range(1, 2**size):
            sum_copy(group, delta).wait_recv()
        total = parts[group, 0]
        for member in range(1, 2**size):
            total = total + parts[group, member]
    norm_ref[...] = jnp.sqrt(total / (devices * width) + 1e-06).reshape(total_rows)

    for level, position, piece in moves:

        @pl.when(sends(level, position))
        def _(level=level, position=position, piece=piece):
            block_copy(level, position, piece).wait_send()

    for level in range(1, depth + 1):
        for index in range(STREAMS):
            up_copy(level, index).wait_send()
    for level in range(1, sharded + 1):
        for index in range(STREAMS):
            down_copy(level, index).wait_send()
    for group, delta, _ in deltas:
        sum_copy(group, delta).wait_send()


def body(right_side, leaf_inverse, leaf_diag, node_block):
    columns = lax.axis_size("col")
    devices = lax.axis_size("row") * columns
    depth = devices.bit_length() - 1
    rows, width = right_side.shape
    half = width // 2
    sharded = 1
    while sharded < depth - 1 and sharded < SHARDED and rows % (2 ** (sharded + 1) * 16 * STREAMS) == 0:
        sharded += 1
    groups = -(-depth // GROUP_BITS)

    def rows_at(level):
        return rows // 2 ** min(level, sharded)

    def vmem(*shape):
        return pltpu.VMEM(shape, jnp.float32)

    dma = pltpu.SemaphoreType.DMA
    scratch = [
        vmem(rows, width),
        vmem(width, width),
        vmem(width, width),
        vmem(depth + 2, width, width),
        vmem(rows, half),
        vmem(groups, 2**GROUP_BITS, 1, rows),
        vmem(groups, 1, rows),
    ]
    scratch += [vmem(rows_at(level), half) for level in range(depth)]
    scratch += [vmem(rows_at(level), half) for level in range(1, depth + 1)]
    scratch += [vmem(rows_at(level), half) for level in range(1, depth)]
    scratch += [vmem(rows_at(level), half) for level in range(sharded)]
    scratch += [vmem(rows_at(level), half) for level in range(1, sharded + 1)]
    scratch += [
        dma((4,)),
        dma((depth + 2, depth, 2 * PIECES)),
        dma((depth + 2, 2 * PIECES)),
        dma((depth + 1, STREAMS)),
        dma((depth + 1, STREAMS)),
        dma((sharded + 1, STREAMS)),
        dma((sharded + 1, STREAMS)),
        dma((groups, 2**GROUP_BITS)),
        dma((groups, 2**GROUP_BITS)),
    ]
    in_hbm = pl.BlockSpec(memory_space=pltpu.HBM)
    in_vmem = pl.BlockSpec(memory_space=pltpu.VMEM)
    arguments = [
        pltpu.with_memory_space_constraint(argument, pltpu.HBM)
        for argument in (right_side, leaf_inverse, leaf_diag, node_block)
    ]
    solved, norm = pl.pallas_call(
        functools.partial(kernel, devices, columns, sharded),
        out_shape=(
            pltpu.VMEM((rows, width), jnp.float32),
            jax.ShapeDtypeStruct((rows,), jnp.float32),
        ),
        in_specs=[in_hbm] * 4,
        out_specs=(in_vmem, in_vmem),
        scratch_shapes=scratch,
        compiler_params=pltpu.CompilerParams(vmem_limit_bytes=16 * 2**20, collective_id=0, has_side_effects=True),
    )(*arguments)
    return (solved, norm)


def solution(mesh):
    return jax.shard_map(
        body,
        mesh=mesh,
        in_specs=(
            P(None, ("row", "col")),
            P(("row", "col"), None, None),
            P(("row", "col"), None, None),
            P(("row", "col"), None, None),
        ),
        out_specs=(P(None, ("row", "col")), P()),
        check_vma=False,
    )
```

time: 49.4 us -> 36.3 us (0.73)
  Pallas kernels: 45.6 us -> 34.2 us
  local copies, waits for them, and re-layouts: 2.43 us -> 1.33 us
  other arithmetic: 0.6 us -> 0 us
    pallas_call x1, Pallas kernels: 45.6 us -> 34.2 us  [body(): pl.pallas_call(functools.partial(kernel, devices, columns, sharded), out_...]
    unnamed x3 -> x2, local copies, waits for them, and re-layouts: 2.43 us -> 1.33 us
    pallas_call x1 -> x0, other arithmetic: 0.6 us -> none  [body(): pl.pallas_call(functools.partial(kernel, devices, columns, sharded), out_...]
where the time goes in v2:
time: 36.3 us; the launch traced here: 36.2 us
  Pallas kernels  34.2 us (94%)
  local copies, waits for them, and re-layouts  1.33 us (4%)
  between operations  0.64 us (2%)
    pallas_call x1, Pallas kernels, body(): pl.pallas_call(functools.partial(kernel, devices, columns, sharded), out_...  34.2 us
    unnamed x2, local copies, waits for them, and re-layouts  1.33 us

profile of v2, /device:TPU:0, one launch (start us, length us, event | category | flops | bytes accessed | tf_op | source)
XLA Modules:
  0.0 36.2 jit_solution(17489311129349277830)
XLA Ops:
  0.6 34.2 %shard_map.59 = (f32[384,256]{1,0:T(8,128)S(1)}, f32[384]{0:T(512)S(1)}) custom-call(f32[384,256]{1,0:T(8,128)} %refs_0_.1, f32[1,256,256]{2,1,0:T(8,128)} %refs_1_.1, f32[1,256,256]{2,1,0:T(8,128)} %refs_2_.1, f32[1,256,256]{2,1,0:T(8,128)} %refs_3_.1), custom_call_target="tpu_custom_call" | custom-call | tf_op jit(solution)/shard_map/pallas_call | solution.py:410
  34.8 0.7 %copy.8 = f32[384,256]{1,0:T(8,128)} copy(f32[384,256]{1,0:T(8,128)S(1)} %get-tuple-element.2) | data formatting | bytes 786432
  35.6 0.6 %copy.9 = f32[384]{0:T(512)} copy(f32[384]{0:T(512)S(1)} %get-tuple-element.7) | data formatting | bytes 3072

commit v3 on v2

--- a/solution.py
+++ b/solution.py
@@ -12,6 +12,7 @@
 GROUP_BITS = 5
 STREAMS = 1
 SHARDED = 1
+TREES = {}
 
 
 def halves(value):
@@ -58,13 +59,15 @@
     upper, lower = range(PIECES), range(PIECES, 2 * PIECES)
     me = lax.axis_index("row") * columns + lax.axis_index("col")
 
+    bits = [lax.rem(lax.div(me, 2**position), 2) for position in range(depth)]
+
     def bit(position):
-        return lax.rem(lax.div(me, 2**position), 2)
+        return bits[position]
 
     def place(index):
         return (lax.div(index, columns), lax.rem(index, columns))
 
-    def flipped(delta):
+    def flip(delta):
         other = me
         for position in range(depth):
             if delta >> position & 1:
@@ -75,6 +78,11 @@
     for first in range(0, depth, GROUP_BITS):
         groups.append((first, min(GROUP_BITS, depth - first)))
     deltas = [(g, d, d << first) for g, (first, size) in enumerate(groups) for d in range(1, 2**size)]
+
+    partners = {delta: flip(delta) for _, _, delta in deltas}
+
+    def flipped(delta):
+        return partners[delta]
 
     slot = jnp.int32(0)
     for position in range(depth):
@@ -94,65 +102,83 @@
             barrier, inc=1, device_id=flipped(1 << position), device_id_type=MESH
         )
 
-    def sends(level, position):
-        if level == 0:
-            return me == 0
-        if position == level - 1:
-            return lax.rem(me, 2**level) == 2 ** (level - 1)
-        return lax.rem(me, 2 ** (position + 1)) == 0
-
-    def receives(level, position):
-        if level == 0:
-            return me == devices // 2
-        if position == level - 1:
-            return lax.rem(me, 2**level) == 0
-        return lax.rem(me, 2 ** (position + 1)) == 2**position
-
-    def block_copy(level, position, piece):
+    orders = {0: [depth - 1], depth: [depth - 1], depth + 1: list(range(depth - 2, -1, -1))}
+    for level in range(1, depth):
+        orders[level] = list(range(level - 1, -1, -1))
+    for level, order in TREES.items():
+        if level < depth:
+            orders[level] = list(order)
+
+    def match(level, phase, moved):
+        held = jnp.int32(0)
+        for place_in_order, position in enumerate(orders[level]):
+            if place_in_order >= phase:
+                owner = int(0 < level <= depth and position == level - 1)
+                if moved and place_in_order == phase:
+                    owner = 1 - owner
+                here = bit(position)
+                held = held + (here if owner == 0 else 1 - here)
+        if level in (0, depth):
+            held = held + lax.rem(me, devices // 2)
+        return held == 0
+
+    match_of = {
+        (level, phase, moved): match(level, phase, moved)
+        for level in orders
+        for phase in range(len(orders[level]))
+        for moved in (False, True)
+    }
+
+    def matches(level, phase, moved):
+        return match_of[level, phase, moved]
+
+    def block_copy(level, phase, piece):
         rows = pl.ds(piece * chunk, chunk)
         return pltpu.make_async_remote_copy(
             src_ref=blocks.at[level, rows],
             dst_ref=blocks.at[level, rows],
-            send_sem=block_send.at[level, position, piece],
+            send_sem=block_send.at[level, phase, piece],
             recv_sem=block_recv.at[level, piece],
-            device_id=flipped(1 << position),
+            device_id=flipped(1 << orders[level][phase]),
             device_id_type=MESH,
         )
 
     moves = []
 
-    def block_start(level, position, piece):
-        moves.append((level, position, piece))
-
-        @pl.when(sends(level, position))
+    def block_start(level, phase, piece):
+        moves.append((level, phase, piece))
+
+        @pl.when(matches(level, phase, False))
         def _():
-            block_copy(level, position, piece).start()
-
-    def block_wait(level, position, piece):
-        @pl.when(receives(level, position))
+            block_copy(level, phase, piece).start()
+
+    def block_wait(level, phase, piece):
+        @pl.when(matches(level, phase, True))
         def _():
-            block_copy(level, position, piece).wait_recv()
+            block_copy(level, phase, piece).wait_recv()
+
+    def last_wait(level, piece):
+        block_wait(level, len(orders[level]) - 1, piece)
 
     def relay(phase, pieces):
         for piece in pieces:
             for level in range(phase, depth):
-                position = level - phase
                 if phase > 1:
-                    block_wait(level, position + 1, piece)
-                block_start(level, position, piece)
+                    block_wait(level, phase - 2, piece)
+                block_start(level, phase - 1, piece)
 
     def relay_root(phase):
         if phase == 1:
             for piece in (*upper, *lower):
-                block_start(depth, depth - 1, piece)
+                block_start(depth, 0, piece)
             for piece in lower:
-                block_start(0, depth - 1, piece)
+                block_start(0, 0, piece)
             return
         if phase == 2:
             for piece in (*upper, *lower):
-                block_wait(depth, depth - 1, piece)
+                block_wait(depth, 0, piece)
             for piece in lower:
-                block_wait(0, depth - 1, piece)
+                block_wait(0, 0, piece)
 
             @pl.when(lax.rem(me, devices // 2) == 0)
             def _():
@@ -161,10 +187,9 @@
                 )
 
         for piece in upper:
-            position = depth - phase
             if phase > 2:
-                block_wait(depth + 1, position + 1, piece)
-            block_start(depth + 1, position, piece)
+                block_wait(depth + 1, phase - 3, piece)
+            block_start(depth + 1, phase - 2, piece)
 
     def rows_at(level):
         return total_rows // 2 ** min(level, sharded)
@@ -230,14 +255,14 @@
 
     def keep(level):
         for piece in upper:
-            block_wait(level, 0, piece)
+            last_wait(level, piece)
         weights = halves(blocks[level, :half])
         for index in range(STREAMS):
             stored[level][stream(level, index), :] = product(joined(level, index), weights, 1)
 
     for level in range(1, depth):
         for piece in lower:
-            block_wait(level, 0, piece)
+            last_wait(level, piece)
         weights = halves(blocks[level, half:])
         for index in range(STREAMS):
             up_copy(level, index).wait_recv()
@@ -256,7 +281,7 @@
     keep(depth - 1)
 
     for piece in upper:
-        block_wait(depth + 1, 0, piece)
+        last_wait(depth + 1, piece)
     root_weights = halves(blocks[depth + 1, :half])
     above = {
         level: halves(blocks[level, :, span(bit(level - 1), half)])
@@ -329,12 +354,28 @@
             device_id_type=MESH,
         )
 
+    def drain():
+        for level, phase, piece in moves:
+
+            @pl.when(matches(level, phase, False))
+            def _(level=level, phase=phase, piece=piece):
+                block_copy(level, phase, piece).wait_send()
+
+        for level in range(1, depth + 1):
+            for index in range(STREAMS):
+                up_copy(level, index).wait_send()
+        for level in range(1, sharded + 1):
+            for index in range(STREAMS):
+                down_copy(level, index).wait_send()
+
     for group, (position, size) in enumerate(groups):
         mine = lax.rem(lax.div(me, 2**position), 2**size)
         sums[group] = total
-        for delta in range(1, 2**size):
+        for delta in reversed(range(1, 2**size)):
             sum_copy(group, delta).start()
         parts[group, mine] = total
+        if group == 0:
+            drain()
         for delta in range(1, 2**size):
             sum_copy(group, delta).wait_recv()
         total = parts[group, 0]
@@ -342,18 +383,6 @@
             total = total + parts[group, member]
     norm_ref[...] = jnp.sqrt(total / (devices * width) + 1e-06).reshape(total_rows)
 
-    for level, position, piece in moves:
-
-        @pl.when(sends(level, position))
-        def _(level=level, position=position, piece=piece):
-            block_copy(level, position, piece).wait_send()
-
-    for level in range(1, depth + 1):
-        for index in range(STREAMS):
-            up_copy(level, index).wait_send()
-    for level in range(1, sharded + 1):
-        for index in range(STREAMS):
-            down_copy(level, index).wait_send()
     for group, delta, _ in deltas:
         sum_copy(group, delta).wait_send()
 

time: 36.3 us -> 36 us (level)
  no operation moved by 1% of the time
where the time goes in v3:
time: 36 us; the launch traced here: 35.8 us
  Pallas kernels  33.9 us (94%)
  local copies, waits for them, and re-layouts  1.33 us (4%)
  between operations  0.64 us (2%)
    pallas_call x1, Pallas kernels, body(): pl.pallas_call(functools.partial(kernel, devices, columns, sharded), out_...  33.9 us
    unnamed x2, local copies, waits for them, and re-layouts  1.33 us

profile of v3, /device:TPU:0, one launch (start us, length us, event | category | flops | bytes accessed | tf_op | source)
XLA Modules:
  0.0 35.8 jit_solution(14731033829948286632)
XLA Ops:
  0.6 33.9 %shard_map.59 = (f32[384,256]{1,0:T(8,128)S(1)}, f32[384]{0:T(512)S(1)}) custom-call(f32[384,256]{1,0:T(8,128)} %refs_0_.1, f32[1,256,256]{2,1,0:T(8,128)} %refs_1_.1, f32[1,256,256]{2,1,0:T(8,128)} %refs_2_.1, f32[1,256,256]{2,1,0:T(8,128)} %refs_3_.1), custom_call_target="tpu_custom_call" | custom-call | tf_op jit(solution)/shard_map/pallas_call | solution.py:439
  34.5 0.7 %copy.8 = f32[384,256]{1,0:T(8,128)} copy(f32[384,256]{1,0:T(8,128)S(1)} %get-tuple-element.2) | data formatting | bytes 786432
  35.3 0.6 %copy.9 = f32[384]{0:T(512)} copy(f32[384]{0:T(512)S(1)} %get-tuple-element.7) | data formatting | bytes 3072
